TPU v7x, 128 devices: a whole 4x4x4 slice. The times are simulated.
128 devices in a mesh: sx: 8 (over y_hi, x), sy: 8 (over z, core), par: 2 (over y_lo).
Axes of the slice: x: 4, y: 4 (y_hi: 2, y_lo: 2; y = y_hi * 2 + y_lo), z: 4, core: 2. Of those that a mesh axis runs over, the one named last changes fastest.
Arguments:
- initial_state: float32 [64, 128, 128, 128], P('par', 'sx', 'sy'), may hold values from -6 to 6
- conductivity: float32 [64, 128, 128, 128], P('par', 'sx', 'sy'), may hold values from 0.1 to 1
- omega: bfloat16 [64, 64], replicated, may hold values from -0.75 to 0.75
- psi: bfloat16 [64, 128, 128, 128], P(None, 'sx', 'sy'), may hold values from -0.01171875 to 0.01171875
- range_prev: bfloat16 [64, 128, 128, 128], P('par', 'sx', 'sy'), may hold values from -3 to 3
- corange_prev: float32 [64, 64], P(None, 'par'), may hold values from -3 to 3
Outputs:
- final_state: float32 [64, 128, 128, 128], P('par', 'sx', 'sy')
- range_sketch: bfloat16 [64, 128, 128, 128], P('par', 'sx', 'sy')
- corange_sketch: float32 [64, 64], P(None, 'par')
All inputs are finite; a program needn't handle non-finite values.
Results may differ from a plain program's by a relative error of at most 0.0033.
Values may be sent and summed in bfloat16 or wider, within the bound.
A program may use at most 192 MiB of HBM per device.

v0:
```python
import jax
import jax.numpy as jnp
from jax import lax
from jax.sharding import PartitionSpec as P

STEPS = 4


def extended(block, sides, width):
    for axis, dim in sides:
        count = lax.axis_size(axis)
        forward = [(i, i + 1) for i in range(count - 1)]
        backward = [(target, source) for source, target in forward]
        low = lax.ppermute(
            lax.slice_in_dim(block, block.shape[dim] - width, None, axis=dim), axis, forward
        )
        high = lax.ppermute(lax.slice_in_dim(block, 0, width, axis=dim), axis, backward)
        block = jnp.concatenate([low, block, high], axis=dim)
    return block


def advance(field, kpad):
    center = field[:, 1:-1, 1:-1, :]
    kcen = kpad[:, 1:-1, 1:-1, :]
    width_x = center.shape[1]
    width_y = center.shape[2]
    zfield = jnp.pad(center, ((0, 0), (0, 0), (0, 0), (1, 1)))
    zcond = jnp.pad(kcen, ((0, 0), (0, 0), (0, 0), (1, 1)))
    length = center.shape[3]
    pairs = [
        (field[:, 2:, 1:-1, :], kpad[:, 2:, 1:-1, :]),
        (field[:, :width_x, 1:-1, :], kpad[:, :width_x, 1:-1, :]),
        (field[:, 1:-1, 2:, :], kpad[:, 1:-1, 2:, :]),
        (field[:, 1:-1, :width_y, :], kpad[:, 1:-1, :width_y, :]),
        (zfield[:, :, :, 2:], zcond[:, :, :, 2:]),
        (zfield[:, :, :, :length], zcond[:, :, :, :length]),
    ]
    total = jnp.zeros_like(center)
    for unb, knb in pairs:
        total = total + 0.5 * (kcen + knb) * (unb - center)
    return center + 0.16 * total


def per_device(initial_state, conductivity, omega, psi, range_prev, corange_prev):
    samples, cells_x, cells_y, length = initial_state.shape
    kpad = extended(conductivity, (("sx", 1), ("sy", 2)), 1)
    state = initial_state
    for step in range(STEPS):
        field = extended(state, (("sx", 1), ("sy", 2)), 1)
        state = advance(field, kpad)
    snapshot = state.astype(jnp.bfloat16)
    flat_snap = snapshot.reshape(samples, cells_x * cells_y * length)
    rank = omega.shape[1]
    rank_dev = range_prev.shape[0]
    own_cols = lax.dynamic_slice_in_dim(omega, lax.axis_index("par") * rank_dev, rank_dev, 1)
    start_sum = range_prev.astype(jnp.float32)
    piece = lax.all_gather(snapshot, "par", axis=0, tiled=True)
    rows = piece.shape[0]
    term = lax.dot_general(
        own_cols,
        piece.reshape(rows, -1),
        (((0,), (0,)), ((), ())),
        preferred_element_type=jnp.float32,
    )
    range_sum = start_sum + term.reshape(start_sum.shape)
    range_sketch = range_sum.astype(jnp.bfloat16)
    flat_psi = psi.reshape(rank, cells_x * cells_y * length)
    partial_value = lax.dot_general(
        flat_psi, flat_snap, (((1,), (1,)), ((), ())), preferred_element_type=jnp.float32
    )
    corange_sketch = corange_prev + lax.psum(partial_value, ("sx", "sy"))
    return (state, range_sketch, corange_sketch)


def solution(mesh):
    in_specs = (
        P("par", "sx", "sy", None),
        P("par", "sx", "sy", None),
        P(),
        P(None, "sx", "sy", None),
        P("par", "sx", "sy", None),
        P(None, "par"),
    )
    out_specs = (P("par", "sx", "sy", None), P("par", "sx", "sy", None), P(None, "par"))
    return jax.shard_map(
        per_device, mesh=mesh, in_specs=in_specs, out_specs=out_specs, check_vma=False
    )
```

profile of v0, /device:TPU:24, one launch (start us, length us, event | category | flops | bytes accessed | tf_op | source)
XLA Modules:
  0.0 525.8 jit_solution(14510973290693297946)
XLA Ops:
  7.2 4.8 copy.22
  12.0 3.4 collective-permute-start.2
  15.5 6.3 %collective-permute-start = (f32[32,1,16,128]{3,0,2,1:T(8,128)S(1)}, f32[32,1,16,128]{3,0,2,1:T(8,128)S(1)}, u32[]{:S(2)}, u32[]{:S(2)}) collective-permute-start(f32[32,1,16,128]{3,0,2,1:T(8,128)S(1)} %get-tuple-element.31), channel_id=1, source_target_pairs={{16,0},{32,16},{48,32},{64,48},{80,64},{96,80},{112,96},{17,1},{33... | collective-permute-start | bytes 786440 | tf_op jit(solution)/shard_map/ppermute | solution.py:17
  21.8 2.4 copy.44
  26.2 7.5 %collective-permute-start.1 = (f32[32,1,16,128]{3,0,2,1:T(8,128)S(1)}, f32[32,1,16,128]{3,0,2,1:T(8,128)S(1)}, u32[]{:S(2)}, u32[]{:S(2)}) collective-permute-start(f32[32,1,16,128]{3,0,2,1:T(8,128)S(1)} %get-tuple-element.32), channel_id=1, source_target_pairs={{16,0},{32,16},{48,32},{64,48},{80,64},{96,80},{112,96},{17,1},{33... | collective-permute-start | bytes 786440 | tf_op jit(solution)/shard_map/ppermute | solution.py:17
  33.8 2.4 constant_dynamic-update-slice_fusion.1
  37.6 3.0 collective-permute-start.6
  41.4 4.4 constant_dynamic-update-slice_fusion.4
  48.9 4.3 collective-permute-start.7
  54.2 10.3 %fusion.9 = f32[32,16,16,128]{3,0,2,1:T(8,128)S(1)} fusion(f32[32,16,16,128]{3,0,2,1:T(8,128)S(1)} %copy.44, f32[32,18,16,128]{3,0,2,1:T(8,128)} %constant_dynamic-update-slice_fusion.3, f32[32,18,1,128]{3,0,2,1:T(8,128)S(1)} %collective-permute-done.7, f32[32,18,1,128]{3,0,2,1:T(8,128)S(1)} %collective-permute-done.5, ...), kind=kLoop, calls=%fused_computation.19 | loop fusion | flops 40894464 | bytes 24248320 | tf_op jit(solution)/shard_map/add | solution.py:41
  66.5 3.9 collective-permute-start.9
  70.4 2.4 collective-permute-done.8
  72.8 5.5 %collective-permute-done.9 = f32[32,1,16,128]{3,0,2,1:T(8,128)S(1)} collective-permute-done((f32[32,1,16,128]{3,0,2,1:T(8,128)S(1)}, f32[32,1,16,128]{3,0,2,1:T(8,128)S(1)}, u32[]{:S(2)}, u32[]{:S(2)}) %collective-permute-start.9) | collective-permute-done | bytes 262176 | tf_op jit(solution)/shard_map/ppermute | solution.py:14
  79.7 5.6 %collective-permute-start.11 = (f32[32,18,1,128]{3,0,2,1:T(8,128)S(1)}, f32[32,18,1,128]{3,0,2,1:T(8,128)S(1)}, u32[]{:S(2)}, u32[]{:S(2)}) collective-permute-start(f32[32,18,1,128]{3,0,2,1:T(8,128)S(1)} %get-tuple-element.19), channel_id=1, source_target_pairs={{0,2},{2,4},{4,6},{6,8},{8,10},{10,12},{12,14},{1,3},{3,5},{5,7},{... | collective-permute-start | bytes 884744 | tf_op jit(solution)/shard_map/ppermute | solution.py:14
  86.5 8.1 %fusion.17 = f32[32,16,16,128]{3,0,2,1:T(8,128)S(1)} fusion(f32[32,16,16,128]{3,0,2,1:T(8,128)S(1)} %fusion.9, f32[32,18,1,128]{3,0,2,1:T(8,128)S(1)} %collective-permute-done.11, f32[32,1,16,128]{3,0,2,1:T(8,128)S(1)} %collective-permute-done.8, f32[32,1,16,128]{3,0,2,1:T(8,128)S(1)} %collective-permute-done.9, ...), kind=kLoop, calls=%fused_computation.27 | loop fusion | flops 45088768 | bytes 19529728 | tf_op jit(solution)/shard_map/add | solution.py:41
  96.5 3.9 collective-permute-start.13
  100.5 2.4 collective-permute-done.12
  102.9 5.5 %collective-permute-done.13 = f32[32,1,16,128]{3,0,2,1:T(8,128)S(1)} collective-permute-done((f32[32,1,16,128]{3,0,2,1:T(8,128)S(1)}, f32[32,1,16,128]{3,0,2,1:T(8,128)S(1)}, u32[]{:S(2)}, u32[]{:S(2)}) %collective-permute-start.13) | collective-permute-done | bytes 262176 | tf_op jit(solution)/shard_map/ppermute | solution.py:14
  109.8 8.9 %collective-permute-start.15 = (f32[32,18,1,128]{3,0,2,1:T(8,128)S(1)}, f32[32,18,1,128]{3,0,2,1:T(8,128)S(1)}, u32[]{:S(2)}, u32[]{:S(2)}) collective-permute-start(f32[32,18,1,128]{3,0,2,1:T(8,128)S(1)} %get-tuple-element.17), channel_id=1, source_target_pairs={{0,2},{2,4},{4,6},{6,8},{8,10},{10,12},{12,14},{1,3},{3,5},{5,7},{... | collective-permute-start | bytes 884744 | tf_op jit(solution)/shard_map/ppermute | solution.py:14
  119.8 8.1 %fusion.25 = f32[32,16,16,128]{3,0,2,1:T(8,128)S(1)} fusion(f32[32,16,16,128]{3,0,2,1:T(8,128)S(1)} %fusion.17, f32[32,18,1,128]{3,0,2,1:T(8,128)S(1)} %collective-permute-done.15, f32[32,1,16,128]{3,0,2,1:T(8,128)S(1)} %collective-permute-done.12, f32[32,1,16,128]{3,0,2,1:T(8,128)S(1)} %collective-permute-done.13, ...), kind=kLoop, calls=%fused_computation.35 | loop fusion | flops 45088768 | bytes 19529728 | tf_op jit(solution)/shard_map/add | solution.py:41
  129.9 3.9 collective-permute-start.17
  133.8 2.4 collective-permute-done.16
  136.2 5.5 %collective-permute-done.17 = f32[32,1,16,128]{3,0,2,1:T(8,128)S(1)} collective-permute-done((f32[32,1,16,128]{3,0,2,1:T(8,128)S(1)}, f32[32,1,16,128]{3,0,2,1:T(8,128)S(1)}, u32[]{:S(2)}, u32[]{:S(2)}) %collective-permute-start.17) | collective-permute-done | bytes 262176 | tf_op jit(solution)/shard_map/ppermute | solution.py:14
  143.1 8.6 %collective-permute-start.19 = (f32[32,18,1,128]{3,0,2,1:T(8,128)S(1)}, f32[32,18,1,128]{3,0,2,1:T(8,128)S(1)}, u32[]{:S(2)}, u32[]{:S(2)}) collective-permute-start(f32[32,18,1,128]{3,0,2,1:T(8,128)S(1)} %get-tuple-element.15), channel_id=1, source_target_pairs={{0,2},{2,4},{4,6},{6,8},{8,10},{10,12},{12,14},{1,3},{3,5},{5,7},{... | collective-permute-start | bytes 884744 | tf_op jit(solution)/shard_map/ppermute | solution.py:14
  152.9 9.7 %fusion.100 = (bf16[32,16,16,128]{3,0,2,1:T(8,128)(2,1)S(1)}, f32[32,16,16,128]{3,0,2,1:T(8,128)}) fusion(f32[32,16,16,128]{3,0,2,1:T(8,128)S(1)} %fusion.25, f32[32,16,16,128]{3,0,2,1:T(8,128)S(1)} %copy.22, f32[32,1,16,128]{3,0,2,1:T(8,128)S(1)} %collective-permute-done.16, f32[32,1,16,128]{3,0,2,1:T(8,128)S(1)} %collective-permute-done.17, ...), kind=kLoop, calls=%fused_computation.155 | loop fusion | flops 46137344 | bytes 21626880 | tf_op jit(solution)/shard_map/convert_element_type | solution.py:51
  162.6 2.1 copy.47
  164.8 6.8 %copy.50 = f32[32,16,16,128]{3,2,1,0:T(8,128)} copy(f32[32,16,16,128]{3,0,2,1:T(8,128)} %get-tuple-element.13) | data formatting | bytes 8388608
  171.6 3.7 fusion.94
  175.3 330.3 %psum.7 = f32[64,32]{0,1:T(8,128)S(1)} all-reduce(f32[64,32]{0,1:T(8,128)S(1)} %fusion.94), channel_id=1, replica_groups=mesh['sx'=8,'sy'=8,'par'=2] {'sx','sy'}, use_global_device_ids=true, to_apply=%region_0.1 | all-reduce | flops 2048 | bytes 16384 | tf_op jit(solution)/shard_map/psum | solution.py:71
  506.2 4.9 copy.69
  512.7 4.1 add_convert_fusion
  516.8 2.1 copy.51
  (54 shorter events, 23.8 us)
Async XLA Ops:
  7.2 505.2 %copy-start = (bf16[64,64]{1,0:T(8,128)(2,1)S(1)}, bf16[64,64]{1,0:T(8,128)(2,1)}, u32[]{:S(2)}) copy-start(bf16[64,64]{1,0:T(8,128)(2,1)} %param.8) | copy-start | bytes 24580
  7.2 499.1 %all-gather.2.cloned.1.call-start = ((), (), s32[]{:S(2)}) async-start(), calls=%async_computation | async-start | bytes 6291456 | tf_op jit(solution)/shard_map/all_gather | solution.py:57
  7.2 14.6 %copy-start.2 = (f32[32,16,16,128]{3,2,1,0:T(8,128)S(1)}, f32[32,16,16,128]{3,2,1,0:T(8,128)}, u32[]{:S(2)}) copy-start(f32[32,16,16,128]{3,2,1,0:T(8,128)} %param.6) | copy-start | bytes 12582916
  12.0 21.7 %collective-permute-start.2 = (f32[32,1,16,128]{3,0,2,1:T(8,128)S(1)}, f32[32,1,16,128]{3,0,2,1:T(8,128)S(1)}, u32[]{:S(2)}, u32[]{:S(2)}) collective-permute-start(f32[32,1,16,128]{3,0,2,1:T(8,128)S(1)} %get-tuple-element.30), channel_id=1, source_target_pairs={{0,16},{16,32},{32,48},{48,64},{64,80},{80,96},{96,112},{1,17},{17... | collective-permute-start | bytes 786440 | tf_op jit(solution)/shard_map/ppermute | solution.py:14
  15.5 18.3 %copy-start.1 = (f32[32,16,16,128]{3,2,1,0:T(8,128)S(1)}, f32[32,16,16,128]{3,2,1,0:T(8,128)}, u32[]{:S(2)}) copy-start(f32[32,16,16,128]{3,2,1,0:T(8,128)} %param.7) | copy-start | bytes 12582916
  15.5 20.8 %collective-permute-start = (f32[32,1,16,128]{3,0,2,1:T(8,128)S(1)}, f32[32,1,16,128]{3,0,2,1:T(8,128)S(1)}, u32[]{:S(2)}, u32[]{:S(2)}) collective-permute-start(f32[32,1,16,128]{3,0,2,1:T(8,128)S(1)} %get-tuple-element.31), channel_id=1, source_target_pairs={{16,0},{32,16},{48,32},{64,48},{80,64},{96,80},{112,96},{17,1},{33... | collective-permute-start | bytes 786440 | tf_op jit(solution)/shard_map/ppermute | solution.py:17
  24.3 16.4 %collective-permute-start.3 = (f32[32,1,16,128]{3,0,2,1:T(8,128)S(1)}, f32[32,1,16,128]{3,0,2,1:T(8,128)S(1)}, u32[]{:S(2)}, u32[]{:S(2)}) collective-permute-start(f32[32,1,16,128]{3,0,2,1:T(8,128)S(1)} %get-tuple-element.33), channel_id=1, source_target_pairs={{0,16},{16,32},{32,48},{48,64},{64,80},{80,96},{96,112},{1,17},{17... | collective-permute-start | bytes 786440 | tf_op jit(solution)/shard_map/ppermute | solution.py:14
  26.2 19.6 %collective-permute-start.1 = (f32[32,1,16,128]{3,0,2,1:T(8,128)S(1)}, f32[32,1,16,128]{3,0,2,1:T(8,128)S(1)}, u32[]{:S(2)}, u32[]{:S(2)}) collective-permute-start(f32[32,1,16,128]{3,0,2,1:T(8,128)S(1)} %get-tuple-element.32), channel_id=1, source_target_pairs={{16,0},{32,16},{48,32},{64,48},{80,64},{96,80},{112,96},{17,1},{33... | collective-permute-start | bytes 786440 | tf_op jit(solution)/shard_map/ppermute | solution.py:17
  36.3 16.9 %collective-permute-start.4 = (f32[32,18,1,128]{3,0,2,1:T(8,128)S(1)}, f32[32,18,1,128]{3,0,2,1:T(8,128)S(1)}, u32[]{:S(2)}, u32[]{:S(2)}) collective-permute-start(f32[32,18,1,128]{3,0,2,1:T(8,128)S(1)} %get-tuple-element.21), channel_id=1, source_target_pairs={{2,0},{4,2},{6,4},{8,6},{10,8},{12,10},{14,12},{3,1},{5,3},{7,5},{... | collective-permute-start | bytes 884744 | tf_op jit(solution)/shard_map/ppermute | solution.py:17
  37.6 15.6 %collective-permute-start.6 = (f32[32,18,1,128]{3,0,2,1:T(8,128)S(1)}, f32[32,18,1,128]{3,0,2,1:T(8,128)S(1)}, u32[]{:S(2)}, u32[]{:S(2)}) collective-permute-start(f32[32,18,1,128]{3,0,2,1:T(8,128)S(1)} %get-tuple-element.20), channel_id=1, source_target_pairs={{0,2},{2,4},{4,6},{6,8},{8,10},{10,12},{12,14},{1,3},{3,5},{5,7},{... | collective-permute-start | bytes 884744 | tf_op jit(solution)/shard_map/ppermute | solution.py:14
  47.6 5.6 %collective-permute-start.5 = (f32[32,18,1,128]{3,0,2,1:T(8,128)S(1)}, f32[32,18,1,128]{3,0,2,1:T(8,128)S(1)}, u32[]{:S(2)}, u32[]{:S(2)}) collective-permute-start(f32[32,18,1,128]{3,0,2,1:T(8,128)S(1)} %get-tuple-element.22), channel_id=1, source_target_pairs={{2,0},{4,2},{6,4},{8,6},{10,8},{12,10},{14,12},{3,1},{5,3},{7,5},{... | collective-permute-start | bytes 884744 | tf_op jit(solution)/shard_map/ppermute | solution.py:17
  48.9 5.3 collective-permute-start.7
  64.5 8.3 %collective-permute-start.8 = (f32[32,1,16,128]{3,0,2,1:T(8,128)S(1)}, f32[32,1,16,128]{3,0,2,1:T(8,128)S(1)}, u32[]{:S(2)}, u32[]{:S(2)}) collective-permute-start(f32[32,1,16,128]{3,0,2,1:T(8,128)S(1)} %get-tuple-element.29), channel_id=1, source_target_pairs={{16,0},{32,16},{48,32},{64,48},{80,64},{96,80},{112,96},{17,1},{33... | collective-permute-start | bytes 786440 | tf_op jit(solution)/shard_map/ppermute | solution.py:17
  66.5 11.9 %collective-permute-start.9 = (f32[32,1,16,128]{3,0,2,1:T(8,128)S(1)}, f32[32,1,16,128]{3,0,2,1:T(8,128)S(1)}, u32[]{:S(2)}, u32[]{:S(2)}) collective-permute-start(f32[32,1,16,128]{3,0,2,1:T(8,128)S(1)} %get-tuple-element.28), channel_id=1, source_target_pairs={{0,16},{16,32},{32,48},{48,64},{64,80},{80,96},{96,112},{1,17},{17... | collective-permute-start | bytes 786440 | tf_op jit(solution)/shard_map/ppermute | solution.py:14
  78.4 6.9 %collective-permute-start.10 = (f32[32,18,1,128]{3,0,2,1:T(8,128)S(1)}, f32[32,18,1,128]{3,0,2,1:T(8,128)S(1)}, u32[]{:S(2)}, u32[]{:S(2)}) collective-permute-start(f32[32,18,1,128]{3,0,2,1:T(8,128)S(1)} %get-tuple-element.18), channel_id=1, source_target_pairs={{2,0},{4,2},{6,4},{8,6},{10,8},{12,10},{14,12},{3,1},{5,3},{7,5},{... | collective-permute-start | bytes 884744 | tf_op jit(solution)/shard_map/ppermute | solution.py:17
  79.7 6.8 %collective-permute-start.11 = (f32[32,18,1,128]{3,0,2,1:T(8,128)S(1)}, f32[32,18,1,128]{3,0,2,1:T(8,128)S(1)}, u32[]{:S(2)}, u32[]{:S(2)}) collective-permute-start(f32[32,18,1,128]{3,0,2,1:T(8,128)S(1)} %get-tuple-element.19), channel_id=1, source_target_pairs={{0,2},{2,4},{4,6},{6,8},{8,10},{10,12},{12,14},{1,3},{3,5},{5,7},{... | collective-permute-start | bytes 884744 | tf_op jit(solution)/shard_map/ppermute | solution.py:14
  94.6 8.3 %collective-permute-start.12 = (f32[32,1,16,128]{3,0,2,1:T(8,128)S(1)}, f32[32,1,16,128]{3,0,2,1:T(8,128)S(1)}, u32[]{:S(2)}, u32[]{:S(2)}) collective-permute-start(f32[32,1,16,128]{3,0,2,1:T(8,128)S(1)} %get-tuple-element.27), channel_id=1, source_target_pairs={{16,0},{32,16},{48,32},{64,48},{80,64},{96,80},{112,96},{17,1},{33... | collective-permute-start | bytes 786440 | tf_op jit(solution)/shard_map/ppermute | solution.py:17
  96.5 11.9 %collective-permute-start.13 = (f32[32,1,16,128]{3,0,2,1:T(8,128)S(1)}, f32[32,1,16,128]{3,0,2,1:T(8,128)S(1)}, u32[]{:S(2)}, u32[]{:S(2)}) collective-permute-start(f32[32,1,16,128]{3,0,2,1:T(8,128)S(1)} %get-tuple-element.26), channel_id=1, source_target_pairs={{0,16},{16,32},{32,48},{48,64},{64,80},{80,96},{96,112},{1,17},{17... | collective-permute-start | bytes 786440 | tf_op jit(solution)/shard_map/ppermute | solution.py:14
  108.5 10.2 %collective-permute-start.14 = (f32[32,18,1,128]{3,0,2,1:T(8,128)S(1)}, f32[32,18,1,128]{3,0,2,1:T(8,128)S(1)}, u32[]{:S(2)}, u32[]{:S(2)}) collective-permute-start(f32[32,18,1,128]{3,0,2,1:T(8,128)S(1)} %get-tuple-element.16), channel_id=1, source_target_pairs={{2,0},{4,2},{6,4},{8,6},{10,8},{12,10},{14,12},{3,1},{5,3},{7,5},{... | collective-permute-start | bytes 884744 | tf_op jit(solution)/shard_map/ppermute | solution.py:17
  109.8 10.1 %collective-permute-start.15 = (f32[32,18,1,128]{3,0,2,1:T(8,128)S(1)}, f32[32,18,1,128]{3,0,2,1:T(8,128)S(1)}, u32[]{:S(2)}, u32[]{:S(2)}) collective-permute-start(f32[32,18,1,128]{3,0,2,1:T(8,128)S(1)} %get-tuple-element.17), channel_id=1, source_target_pairs={{0,2},{2,4},{4,6},{6,8},{8,10},{10,12},{12,14},{1,3},{3,5},{5,7},{... | collective-permute-start | bytes 884744 | tf_op jit(solution)/shard_map/ppermute | solution.py:14
  128.0 8.3 %collective-permute-start.16 = (f32[32,1,16,128]{3,0,2,1:T(8,128)S(1)}, f32[32,1,16,128]{3,0,2,1:T(8,128)S(1)}, u32[]{:S(2)}, u32[]{:S(2)}) collective-permute-start(f32[32,1,16,128]{3,0,2,1:T(8,128)S(1)} %get-tuple-element.25), channel_id=1, source_target_pairs={{16,0},{32,16},{48,32},{64,48},{80,64},{96,80},{112,96},{17,1},{33... | collective-permute-start | bytes 786440 | tf_op jit(solution)/shard_map/ppermute | solution.py:17
  129.9 11.9 %collective-permute-start.17 = (f32[32,1,16,128]{3,0,2,1:T(8,128)S(1)}, f32[32,1,16,128]{3,0,2,1:T(8,128)S(1)}, u32[]{:S(2)}, u32[]{:S(2)}) collective-permute-start(f32[32,1,16,128]{3,0,2,1:T(8,128)S(1)} %get-tuple-element.24), channel_id=1, source_target_pairs={{0,16},{16,32},{32,48},{48,64},{64,80},{80,96},{96,112},{1,17},{17... | collective-permute-start | bytes 786440 | tf_op jit(solution)/shard_map/ppermute | solution.py:14
  141.8 9.9 %collective-permute-start.18 = (f32[32,18,1,128]{3,0,2,1:T(8,128)S(1)}, f32[32,18,1,128]{3,0,2,1:T(8,128)S(1)}, u32[]{:S(2)}, u32[]{:S(2)}) collective-permute-start(f32[32,18,1,128]{3,0,2,1:T(8,128)S(1)} %get-tuple-element.14), channel_id=1, source_target_pairs={{2,0},{4,2},{6,4},{8,6},{10,8},{12,10},{14,12},{3,1},{5,3},{7,5},{... | collective-permute-start | bytes 884744 | tf_op jit(solution)/shard_map/ppermute | solution.py:17
  143.1 9.8 %collective-permute-start.19 = (f32[32,18,1,128]{3,0,2,1:T(8,128)S(1)}, f32[32,18,1,128]{3,0,2,1:T(8,128)S(1)}, u32[]{:S(2)}, u32[]{:S(2)}) collective-permute-start(f32[32,18,1,128]{3,0,2,1:T(8,128)S(1)} %get-tuple-element.15), channel_id=1, source_target_pairs={{0,2},{2,4},{4,6},{6,8},{8,10},{10,12},{12,14},{1,3},{3,5},{5,7},{... | collective-permute-start | bytes 884744 | tf_op jit(solution)/shard_map/ppermute | solution.py:14
  164.8 6.8 %copy-start.5 = (bf16[64,16,16,128]{3,2,1,0:T(8,128)(2,1)S(1)}, bf16[64,16,16,128]{3,2,1,0:T(8,128)(2,1)}, u32[]{:S(2)}) copy-start(bf16[64,16,16,128]{3,2,1,0:T(8,128)(2,1)} %param.9) | copy-start | bytes 12582916
  171.6 334.0 %copy-start.4 = (f32[64,32]{0,1:T(8,128)S(1)}, f32[64,32]{0,1:T(8,128)}, u32[]{:S(2)}) copy-start(f32[64,32]{0,1:T(8,128)} %param.11) | copy-start | bytes 24580
  511.1 1.6 copy-start.3
Sparse Core Ops, SparseCore 0:
  164.9 63.2 all-gather.1
where the time goes:
time: 527 us; the launch traced here: 526 us
  blocking collectives  330 us (63%)
  starting transfers between devices  73.6 us (14%)
  other arithmetic  36.9 us (7%)
  local copies, waits for them, and re-layouts  34.4 us (7%)
  waiting for transfers between devices  28.3 us (5%)
  between operations  14.5 us (3%)
  matrix products  7.84 us (1%)
    psum x1, blocking collectives, per_device(): corange_sketch = corange_prev + lax.psum(partial_value, ('sx', 'sy'))  330 us
    ppermute x10, starting transfers between devices, extended(): lax.ppermute(lax.slice_in_dim(block, block.shape[dim] - width, None, axis...  47.4 us
    unnamed x22, local copies, waits for them, and re-layouts  30.2 us
    add x3, other arithmetic, advance(): return center + 0.16 * total  26.5 us
    ppermute x10, starting transfers between devices, extended(): lax.ppermute(lax.slice_in_dim(block, 0, width, axis=dim), axis, backward)  26.1 us
    ppermute x10, waiting for transfers between devices, extended(): lax.ppermute(lax.slice_in_dim(block, block.shape[dim] - width, None, axis...  21.1 us
  transfers between devices with their start and end apart: 21, of which 10 were waited for; matrix products, arithmetic and copies ran while one was open for 4% of the time, Pallas kernels for 0%

commit v1 on v0

--- a/solution.py
+++ b/solution.py
@@ -2,6 +2,7 @@
 import jax.numpy as jnp
 from jax import lax
 from jax.sharding import PartitionSpec as P
+from jax.lax import all_gather
 
 STEPS = 4
 
@@ -68,7 +69,7 @@
     partial_value = lax.dot_general(
         flat_psi, flat_snap, (((1,), (1,)), ((), ())), preferred_element_type=jnp.float32
     )
-    corange_sketch = corange_prev + lax.psum(partial_value, ("sx", "sy"))
+    corange_sketch = corange_prev + all_gather(partial_value, axis_name=("sx", "sy")).sum(axis=0)
     return (state, range_sketch, corange_sketch)
 
 

time: 527 us -> 297 us (0.56)
  blocking collectives: 330 us -> 100 us
    psum x1 -> x0, blocking collectives: 330 us -> none  [per_device(): corange_sketch = corange_prev + lax.psum(partial_value, ('sx', 'sy'))]
    all_gather x0 -> x1, blocking collectives: none -> 100 us  [per_device(): all_gather(partial_value, axis_name=('sx', 'sy')).sum(axis=0)]
  transfers between devices with their start and end apart: 21 -> 21, of which waited for: 10 -> 10; matrix products, arithmetic and copies ran while one was open for 4% -> 8% of each run, Pallas kernels for 0% -> 0%
where the time goes in v1:
time: 297 us; the launch traced here: 296 us
  blocking collectives  100 us (34%)
  starting transfers between devices  73.6 us (25%)
  other arithmetic  37 us (12%)
  local copies, waits for them, and re-layouts  34.4 us (12%)
  waiting for transfers between devices  28.3 us (10%)
  between operations  14.5 us (5%)
  matrix products  7.84 us (3%)
    all_gather x1, blocking collectives, per_device(): all_gather(partial_value, axis_name=('sx', 'sy')).sum(axis=0)  100 us
    ppermute x10, starting transfers between devices, extended(): lax.ppermute(lax.slice_in_dim(block, block.shape[dim] - width, None, axis...  47.4 us
    unnamed x22, local copies, waits for them, and re-layouts  30.2 us
    add x3, other arithmetic, advance(): return center + 0.16 * total  26.5 us
    ppermute x10, starting transfers between devices, extended(): lax.ppermute(lax.slice_in_dim(block, 0, width, axis=dim), axis, backward)  26.1 us
    ppermute x10, waiting for transfers between devices, extended(): lax.ppermute(lax.slice_in_dim(block, block.shape[dim] - width, None, axis...  21.1 us
    convert_element_type x1, other arithmetic, per_device(): snapshot = state.astype(jnp.bfloat16)  9.73 us
    ppermute x10, waiting for transfers between devices, extended(): lax.ppermute(lax.slice_in_dim(block, 0, width, axis=dim), axis, backward)  7.24 us
  transfers between devices with their start and end apart: 21, of which 10 were waited for; matrix products, arithmetic and copies ran while one was open for 8% of the time, Pallas kernels for 0%

profile of v1, /device:TPU:24, one launch (start us, length us, event | category | flops | bytes accessed | tf_op | source)
XLA Modules:
  0.0 296.1 jit_solution(2510224462174614220)
XLA Ops:
  7.2 4.8 %copy.22 = f32[32,16,16,128]{3,0,2,1:T(8,128)S(1)} copy(f32[32,16,16,128]{3,2,1,0:T(8,128)} %param.7) | data formatting | bytes 8388608 | tf_op args[1]
  12.0 3.4 %collective-permute-start.2 = (f32[32,1,16,128]{3,0,2,1:T(8,128)S(1)}, f32[32,1,16,128]{3,0,2,1:T(8,128)S(1)}, u32[]{:S(2)}, u32[]{:S(2)}) collective-permute-start(f32[32,1,16,128]{3,0,2,1:T(8,128)S(1)} %get-tuple-element.30), channel_id=1, source_target_pairs={{0,16},{16,32},{32,48},{48,64},{64,80},{80,96},{96,112},{1,17},{17... | collective-permute-start | bytes 786440 | tf_op jit(solution)/shard_map/ppermute | solution.py:15
  15.5 6.3 %collective-permute-start = (f32[32,1,16,128]{3,0,2,1:T(8,128)S(1)}, f32[32,1,16,128]{3,0,2,1:T(8,128)S(1)}, u32[]{:S(2)}, u32[]{:S(2)}) collective-permute-start(f32[32,1,16,128]{3,0,2,1:T(8,128)S(1)} %get-tuple-element.31), channel_id=1, source_target_pairs={{16,0},{32,16},{48,32},{64,48},{80,64},{96,80},{112,96},{17,1},{33... | collective-permute-start | bytes 786440 | tf_op jit(solution)/shard_map/ppermute | solution.py:18
  21.8 2.4 copy.44
  26.2 7.5 %collective-permute-start.1 = (f32[32,1,16,128]{3,0,2,1:T(8,128)S(1)}, f32[32,1,16,128]{3,0,2,1:T(8,128)S(1)}, u32[]{:S(2)}, u32[]{:S(2)}) collective-permute-start(f32[32,1,16,128]{3,0,2,1:T(8,128)S(1)} %get-tuple-element.32), channel_id=1, source_target_pairs={{16,0},{32,16},{48,32},{64,48},{80,64},{96,80},{112,96},{17,1},{33... | collective-permute-start | bytes 786440 | tf_op jit(solution)/shard_map/ppermute | solution.py:18
  33.8 2.4 constant_dynamic-update-slice_fusion.1
  37.6 3.0 %collective-permute-start.6 = (f32[32,18,1,128]{3,0,2,1:T(8,128)S(1)}, f32[32,18,1,128]{3,0,2,1:T(8,128)S(1)}, u32[]{:S(2)}, u32[]{:S(2)}) collective-permute-start(f32[32,18,1,128]{3,0,2,1:T(8,128)S(1)} %get-tuple-element.20), channel_id=1, source_target_pairs={{0,2},{2,4},{4,6},{6,8},{8,10},{10,12},{12,14},{1,3},{3,5},{5,7},{... | collective-permute-start | bytes 884744 | tf_op jit(solution)/shard_map/ppermute | solution.py:15
  41.4 4.4 %constant_dynamic-update-slice_fusion.4 = f32[32,18,16,128]{3,0,2,1:T(8,128)} fusion(f32[32,18,16,128]{3,0,2,1:T(8,128)} %constant_dynamic-update-slice_fusion.5, f32[32,16,16,128]{3,2,1,0:T(8,128)S(1)} %copy-done.2), kind=kLoop, calls=%fused_computation.152 | loop fusion | bytes 8388608
  48.9 4.3 %collective-permute-start.7 = (f32[32,18,1,128]{3,0,2,1:T(8,128)S(1)}, f32[32,18,1,128]{3,0,2,1:T(8,128)S(1)}, u32[]{:S(2)}, u32[]{:S(2)}) collective-permute-start(f32[32,18,1,128]{3,0,2,1:T(8,128)S(1)} %get-tuple-element.23), channel_id=1, source_target_pairs={{0,2},{2,4},{4,6},{6,8},{8,10},{10,12},{12,14},{1,3},{3,5},{5,7},{... | collective-permute-start | bytes 884744 | tf_op jit(solution)/shard_map/ppermute | solution.py:15
  54.2 10.3 %fusion.9 = f32[32,16,16,128]{3,0,2,1:T(8,128)S(1)} fusion(f32[32,16,16,128]{3,0,2,1:T(8,128)S(1)} %copy.44, f32[32,18,16,128]{3,0,2,1:T(8,128)} %constant_dynamic-update-slice_fusion.3, f32[32,18,1,128]{3,0,2,1:T(8,128)S(1)} %collective-permute-done.7, f32[32,18,1,128]{3,0,2,1:T(8,128)S(1)} %collective-permute-done.5, ...), kind=kLoop, calls=%fused_computation.19 | loop fusion | flops 40894464 | bytes 24248320 | tf_op jit(solution)/shard_map/add | solution.py:42
  66.5 3.9 %collective-permute-start.9 = (f32[32,1,16,128]{3,0,2,1:T(8,128)S(1)}, f32[32,1,16,128]{3,0,2,1:T(8,128)S(1)}, u32[]{:S(2)}, u32[]{:S(2)}) collective-permute-start(f32[32,1,16,128]{3,0,2,1:T(8,128)S(1)} %get-tuple-element.28), channel_id=1, source_target_pairs={{0,16},{16,32},{32,48},{48,64},{64,80},{80,96},{96,112},{1,17},{17... | collective-permute-start | bytes 786440 | tf_op jit(solution)/shard_map/ppermute | solution.py:15
  70.4 2.4 collective-permute-done.8
  72.8 5.5 %collective-permute-done.9 = f32[32,1,16,128]{3,0,2,1:T(8,128)S(1)} collective-permute-done((f32[32,1,16,128]{3,0,2,1:T(8,128)S(1)}, f32[32,1,16,128]{3,0,2,1:T(8,128)S(1)}, u32[]{:S(2)}, u32[]{:S(2)}) %collective-permute-start.9) | collective-permute-done | bytes 262176 | tf_op jit(solution)/shard_map/ppermute | solution.py:15
  79.7 5.6 %collective-permute-start.11 = (f32[32,18,1,128]{3,0,2,1:T(8,128)S(1)}, f32[32,18,1,128]{3,0,2,1:T(8,128)S(1)}, u32[]{:S(2)}, u32[]{:S(2)}) collective-permute-start(f32[32,18,1,128]{3,0,2,1:T(8,128)S(1)} %get-tuple-element.19), channel_id=1, source_target_pairs={{0,2},{2,4},{4,6},{6,8},{8,10},{10,12},{12,14},{1,3},{3,5},{5,7},{... | collective-permute-start | bytes 884744 | tf_op jit(solution)/shard_map/ppermute | solution.py:15
  86.5 8.1 %fusion.17 = f32[32,16,16,128]{3,0,2,1:T(8,128)S(1)} fusion(f32[32,16,16,128]{3,0,2,1:T(8,128)S(1)} %fusion.9, f32[32,18,1,128]{3,0,2,1:T(8,128)S(1)} %collective-permute-done.11, f32[32,1,16,128]{3,0,2,1:T(8,128)S(1)} %collective-permute-done.8, f32[32,1,16,128]{3,0,2,1:T(8,128)S(1)} %collective-permute-done.9, ...), kind=kLoop, calls=%fused_computation.27 | loop fusion | flops 45088768 | bytes 19529728 | tf_op jit(solution)/shard_map/add | solution.py:42
  96.5 3.9 %collective-permute-start.13 = (f32[32,1,16,128]{3,0,2,1:T(8,128)S(1)}, f32[32,1,16,128]{3,0,2,1:T(8,128)S(1)}, u32[]{:S(2)}, u32[]{:S(2)}) collective-permute-start(f32[32,1,16,128]{3,0,2,1:T(8,128)S(1)} %get-tuple-element.26), channel_id=1, source_target_pairs={{0,16},{16,32},{32,48},{48,64},{64,80},{80,96},{96,112},{1,17},{17... | collective-permute-start | bytes 786440 | tf_op jit(solution)/shard_map/ppermute | solution.py:15
  100.5 2.4 collective-permute-done.12
  102.9 5.5 %collective-permute-done.13 = f32[32,1,16,128]{3,0,2,1:T(8,128)S(1)} collective-permute-done((f32[32,1,16,128]{3,0,2,1:T(8,128)S(1)}, f32[32,1,16,128]{3,0,2,1:T(8,128)S(1)}, u32[]{:S(2)}, u32[]{:S(2)}) %collective-permute-start.13) | collective-permute-done | bytes 262176 | tf_op jit(solution)/shard_map/ppermute | solution.py:15
  109.8 8.9 %collective-permute-start.15 = (f32[32,18,1,128]{3,0,2,1:T(8,128)S(1)}, f32[32,18,1,128]{3,0,2,1:T(8,128)S(1)}, u32[]{:S(2)}, u32[]{:S(2)}) collective-permute-start(f32[32,18,1,128]{3,0,2,1:T(8,128)S(1)} %get-tuple-element.17), channel_id=1, source_target_pairs={{0,2},{2,4},{4,6},{6,8},{8,10},{10,12},{12,14},{1,3},{3,5},{5,7},{... | collective-permute-start | bytes 884744 | tf_op jit(solution)/shard_map/ppermute | solution.py:15
  119.8 8.1 %fusion.25 = f32[32,16,16,128]{3,0,2,1:T(8,128)S(1)} fusion(f32[32,16,16,128]{3,0,2,1:T(8,128)S(1)} %fusion.17, f32[32,18,1,128]{3,0,2,1:T(8,128)S(1)} %collective-permute-done.15, f32[32,1,16,128]{3,0,2,1:T(8,128)S(1)} %collective-permute-done.12, f32[32,1,16,128]{3,0,2,1:T(8,128)S(1)} %collective-permute-done.13, ...), kind=kLoop, calls=%fused_computation.35 | loop fusion | flops 45088768 | bytes 19529728 | tf_op jit(solution)/shard_map/add | solution.py:42
  129.9 3.9 %collective-permute-start.17 = (f32[32,1,16,128]{3,0,2,1:T(8,128)S(1)}, f32[32,1,16,128]{3,0,2,1:T(8,128)S(1)}, u32[]{:S(2)}, u32[]{:S(2)}) collective-permute-start(f32[32,1,16,128]{3,0,2,1:T(8,128)S(1)} %get-tuple-element.24), channel_id=1, source_target_pairs={{0,16},{16,32},{32,48},{48,64},{64,80},{80,96},{96,112},{1,17},{17... | collective-permute-start | bytes 786440 | tf_op jit(solution)/shard_map/ppermute | solution.py:15
  133.8 2.4 collective-permute-done.16
  136.2 5.5 %collective-permute-done.17 = f32[32,1,16,128]{3,0,2,1:T(8,128)S(1)} collective-permute-done((f32[32,1,16,128]{3,0,2,1:T(8,128)S(1)}, f32[32,1,16,128]{3,0,2,1:T(8,128)S(1)}, u32[]{:S(2)}, u32[]{:S(2)}) %collective-permute-start.17) | collective-permute-done | bytes 262176 | tf_op jit(solution)/shard_map/ppermute | solution.py:15
  143.1 8.6 %collective-permute-start.19 = (f32[32,18,1,128]{3,0,2,1:T(8,128)S(1)}, f32[32,18,1,128]{3,0,2,1:T(8,128)S(1)}, u32[]{:S(2)}, u32[]{:S(2)}) collective-permute-start(f32[32,18,1,128]{3,0,2,1:T(8,128)S(1)} %get-tuple-element.15), channel_id=1, source_target_pairs={{0,2},{2,4},{4,6},{6,8},{8,10},{10,12},{12,14},{1,3},{3,5},{5,7},{... | collective-permute-start | bytes 884744 | tf_op jit(solution)/shard_map/ppermute | solution.py:15
  152.9 9.7 %fusion.100 = (bf16[32,16,16,128]{3,0,2,1:T(8,128)(2,1)S(1)}, f32[32,16,16,128]{3,0,2,1:T(8,128)}) fusion(f32[32,16,16,128]{3,0,2,1:T(8,128)S(1)} %fusion.25, f32[32,16,16,128]{3,0,2,1:T(8,128)S(1)} %copy.22, f32[32,1,16,128]{3,0,2,1:T(8,128)S(1)} %collective-permute-done.16, f32[32,1,16,128]{3,0,2,1:T(8,128)S(1)} %collective-permute-done.17, ...), kind=kLoop, calls=%fused_computation.155 | loop fusion | flops 46137344 | bytes 21626880 | tf_op jit(solution)/shard_map/convert_element_type | solution.py:52
  162.6 2.1 copy.47
  164.8 6.8 %copy.50 = f32[32,16,16,128]{3,2,1,0:T(8,128)} copy(f32[32,16,16,128]{3,0,2,1:T(8,128)} %get-tuple-element.13) | data formatting | bytes 8388608
  171.6 3.7 %fusion.94 = f32[1,64,32]{1,2,0:T(8,128)S(1)} fusion(bf16[32,16,16,128]{3,0,2,1:T(8,128)(2,1)S(1)} %get-tuple-element.12, bf16[64,16,16,128]{3,2,1,0:T(8,128)(2,1)S(1)} %copy-done.5), kind=kOutput, calls=%fused_computation.136 | convolution fusion | flops 134217728 | bytes 6299648 | tf_op jit(solution)/shard_map/dot_general | solution.py:69
  175.3 100.5 %all-gather.1 = f32[64,64,32]{1,2,0:T(8,128)S(1)} all-gather(f32[1,64,32]{1,2,0:T(8,128)S(1)} %fusion.94), channel_id=2, replica_groups=mesh['sx'=8,'sy'=8,'par'=2] {'sx','sy'}, dimensions={0}, use_global_device_ids=true | all-gather | bytes 532480 | tf_op jit(solution)/shard_map/all_gather | solution.py:72
  276.5 4.9 %copy.69 = bf16[8,8,256,128]{3,1,2,0:T(8,128)(2,1)S(1)} copy(bf16[8,8,256,128]{3,2,1,0:T(8,128)(2,1)} %bitcast.29) | data formatting | bytes 8388608
  283.0 4.1 %add_convert_fusion = bf16[32,16,16,128]{3,0,2,1:T(8,128)(2,1)S(1)} fusion(bf16[16,16,128,64]{2,1,0,3:T(8,128)(2,1)S(1)} %bitcast.28, bf16[32,16,16,128]{3,2,1,0:T(8,128)(2,1)S(1)} %copy-done.3, bf16[64,64]{1,0:T(8,128)(2,1)S(1)} %copy-done, s32[]{:T(128)S(6)} %select_n.3), kind=kOutput, calls=%fused_computation.135 | convolution fusion | flops 137363456 | bytes 8396804 | tf_op jit(solution)/shard_map/dot_general | solution.py:60
  287.1 2.1 copy.51
  (55 shorter events, 23.9 us)
Async XLA Ops:
  7.2 275.4 %copy-start = (bf16[64,64]{1,0:T(8,128)(2,1)S(1)}, bf16[64,64]{1,0:T(8,128)(2,1)}, u32[]{:S(2)}) copy-start(bf16[64,64]{1,0:T(8,128)(2,1)} %param.8) | copy-start | bytes 24580
  7.2 269.3 %all-gather.4.cloned.1.call-start = ((), (), s32[]{:S(2)}) async-start(), calls=%async_computation | async-start | bytes 6291456 | tf_op jit(solution)/shard_map/all_gather | solution.py:58
  7.2 14.6 %copy-start.2 = (f32[32,16,16,128]{3,2,1,0:T(8,128)S(1)}, f32[32,16,16,128]{3,2,1,0:T(8,128)}, u32[]{:S(2)}) copy-start(f32[32,16,16,128]{3,2,1,0:T(8,128)} %param.6) | copy-start | bytes 12582916
  12.0 21.7 %collective-permute-start.2 = (f32[32,1,16,128]{3,0,2,1:T(8,128)S(1)}, f32[32,1,16,128]{3,0,2,1:T(8,128)S(1)}, u32[]{:S(2)}, u32[]{:S(2)}) collective-permute-start(f32[32,1,16,128]{3,0,2,1:T(8,128)S(1)} %get-tuple-element.30), channel_id=1, source_target_pairs={{0,16},{16,32},{32,48},{48,64},{64,80},{80,96},{96,112},{1,17},{17... | collective-permute-start | bytes 786440 | tf_op jit(solution)/shard_map/ppermute | solution.py:15
  15.5 18.3 %copy-start.1 = (f32[32,16,16,128]{3,2,1,0:T(8,128)S(1)}, f32[32,16,16,128]{3,2,1,0:T(8,128)}, u32[]{:S(2)}) copy-start(f32[32,16,16,128]{3,2,1,0:T(8,128)} %param.7) | copy-start | bytes 12582916
  15.5 20.8 %collective-permute-start = (f32[32,1,16,128]{3,0,2,1:T(8,128)S(1)}, f32[32,1,16,128]{3,0,2,1:T(8,128)S(1)}, u32[]{:S(2)}, u32[]{:S(2)}) collective-permute-start(f32[32,1,16,128]{3,0,2,1:T(8,128)S(1)} %get-tuple-element.31), channel_id=1, source_target_pairs={{16,0},{32,16},{48,32},{64,48},{80,64},{96,80},{112,96},{17,1},{33... | collective-permute-start | bytes 786440 | tf_op jit(solution)/shard_map/ppermute | solution.py:18
  24.3 16.4 %collective-permute-start.3 = (f32[32,1,16,128]{3,0,2,1:T(8,128)S(1)}, f32[32,1,16,128]{3,0,2,1:T(8,128)S(1)}, u32[]{:S(2)}, u32[]{:S(2)}) collective-permute-start(f32[32,1,16,128]{3,0,2,1:T(8,128)S(1)} %get-tuple-element.33), channel_id=1, source_target_pairs={{0,16},{16,32},{32,48},{48,64},{64,80},{80,96},{96,112},{1,17},{17... | collective-permute-start | bytes 786440 | tf_op jit(solution)/shard_map/ppermute | solution.py:15
  26.2 19.6 %collective-permute-start.1 = (f32[32,1,16,128]{3,0,2,1:T(8,128)S(1)}, f32[32,1,16,128]{3,0,2,1:T(8,128)S(1)}, u32[]{:S(2)}, u32[]{:S(2)}) collective-permute-start(f32[32,1,16,128]{3,0,2,1:T(8,128)S(1)} %get-tuple-element.32), channel_id=1, source_target_pairs={{16,0},{32,16},{48,32},{64,48},{80,64},{96,80},{112,96},{17,1},{33... | collective-permute-start | bytes 786440 | tf_op jit(solution)/shard_map/ppermute | solution.py:18
  36.3 16.9 %collective-permute-start.4 = (f32[32,18,1,128]{3,0,2,1:T(8,128)S(1)}, f32[32,18,1,128]{3,0,2,1:T(8,128)S(1)}, u32[]{:S(2)}, u32[]{:S(2)}) collective-permute-start(f32[32,18,1,128]{3,0,2,1:T(8,128)S(1)} %get-tuple-element.21), channel_id=1, source_target_pairs={{2,0},{4,2},{6,4},{8,6},{10,8},{12,10},{14,12},{3,1},{5,3},{7,5},{... | collective-permute-start | bytes 884744 | tf_op jit(solution)/shard_map/ppermute | solution.py:18
  37.6 15.6 %collective-permute-start.6 = (f32[32,18,1,128]{3,0,2,1:T(8,128)S(1)}, f32[32,18,1,128]{3,0,2,1:T(8,128)S(1)}, u32[]{:S(2)}, u32[]{:S(2)}) collective-permute-start(f32[32,18,1,128]{3,0,2,1:T(8,128)S(1)} %get-tuple-element.20), channel_id=1, source_target_pairs={{0,2},{2,4},{4,6},{6,8},{8,10},{10,12},{12,14},{1,3},{3,5},{5,7},{... | collective-permute-start | bytes 884744 | tf_op jit(solution)/shard_map/ppermute | solution.py:15
  47.6 5.6 %collective-permute-start.5 = (f32[32,18,1,128]{3,0,2,1:T(8,128)S(1)}, f32[32,18,1,128]{3,0,2,1:T(8,128)S(1)}, u32[]{:S(2)}, u32[]{:S(2)}) collective-permute-start(f32[32,18,1,128]{3,0,2,1:T(8,128)S(1)} %get-tuple-element.22), channel_id=1, source_target_pairs={{2,0},{4,2},{6,4},{8,6},{10,8},{12,10},{14,12},{3,1},{5,3},{7,5},{... | collective-permute-start | bytes 884744 | tf_op jit(solution)/shard_map/ppermute | solution.py:18
  48.9 5.3 %collective-permute-start.7 = (f32[32,18,1,128]{3,0,2,1:T(8,128)S(1)}, f32[32,18,1,128]{3,0,2,1:T(8,128)S(1)}, u32[]{:S(2)}, u32[]{:S(2)}) collective-permute-start(f32[32,18,1,128]{3,0,2,1:T(8,128)S(1)} %get-tuple-element.23), channel_id=1, source_target_pairs={{0,2},{2,4},{4,6},{6,8},{8,10},{10,12},{12,14},{1,3},{3,5},{5,7},{... | collective-permute-start | bytes 884744 | tf_op jit(solution)/shard_map/ppermute | solution.py:15
  64.5 8.3 %collective-permute-start.8 = (f32[32,1,16,128]{3,0,2,1:T(8,128)S(1)}, f32[32,1,16,128]{3,0,2,1:T(8,128)S(1)}, u32[]{:S(2)}, u32[]{:S(2)}) collective-permute-start(f32[32,1,16,128]{3,0,2,1:T(8,128)S(1)} %get-tuple-element.29), channel_id=1, source_target_pairs={{16,0},{32,16},{48,32},{64,48},{80,64},{96,80},{112,96},{17,1},{33... | collective-permute-start | bytes 786440 | tf_op jit(solution)/shard_map/ppermute | solution.py:18
  66.5 11.9 %collective-permute-start.9 = (f32[32,1,16,128]{3,0,2,1:T(8,128)S(1)}, f32[32,1,16,128]{3,0,2,1:T(8,128)S(1)}, u32[]{:S(2)}, u32[]{:S(2)}) collective-permute-start(f32[32,1,16,128]{3,0,2,1:T(8,128)S(1)} %get-tuple-element.28), channel_id=1, source_target_pairs={{0,16},{16,32},{32,48},{48,64},{64,80},{80,96},{96,112},{1,17},{17... | collective-permute-start | bytes 786440 | tf_op jit(solution)/shard_map/ppermute | solution.py:15
  78.4 6.9 %collective-permute-start.10 = (f32[32,18,1,128]{3,0,2,1:T(8,128)S(1)}, f32[32,18,1,128]{3,0,2,1:T(8,128)S(1)}, u32[]{:S(2)}, u32[]{:S(2)}) collective-permute-start(f32[32,18,1,128]{3,0,2,1:T(8,128)S(1)} %get-tuple-element.18), channel_id=1, source_target_pairs={{2,0},{4,2},{6,4},{8,6},{10,8},{12,10},{14,12},{3,1},{5,3},{7,5},{... | collective-permute-start | bytes 884744 | tf_op jit(solution)/shard_map/ppermute | solution.py:18
  79.7 6.8 %collective-permute-start.11 = (f32[32,18,1,128]{3,0,2,1:T(8,128)S(1)}, f32[32,18,1,128]{3,0,2,1:T(8,128)S(1)}, u32[]{:S(2)}, u32[]{:S(2)}) collective-permute-start(f32[32,18,1,128]{3,0,2,1:T(8,128)S(1)} %get-tuple-element.19), channel_id=1, source_target_pairs={{0,2},{2,4},{4,6},{6,8},{8,10},{10,12},{12,14},{1,3},{3,5},{5,7},{... | collective-permute-start | bytes 884744 | tf_op jit(solution)/shard_map/ppermute | solution.py:15
  94.6 8.3 %collective-permute-start.12 = (f32[32,1,16,128]{3,0,2,1:T(8,128)S(1)}, f32[32,1,16,128]{3,0,2,1:T(8,128)S(1)}, u32[]{:S(2)}, u32[]{:S(2)}) collective-permute-start(f32[32,1,16,128]{3,0,2,1:T(8,128)S(1)} %get-tuple-element.27), channel_id=1, source_target_pairs={{16,0},{32,16},{48,32},{64,48},{80,64},{96,80},{112,96},{17,1},{33... | collective-permute-start | bytes 786440 | tf_op jit(solution)/shard_map/ppermute | solution.py:18
  96.5 11.9 %collective-permute-start.13 = (f32[32,1,16,128]{3,0,2,1:T(8,128)S(1)}, f32[32,1,16,128]{3,0,2,1:T(8,128)S(1)}, u32[]{:S(2)}, u32[]{:S(2)}) collective-permute-start(f32[32,1,16,128]{3,0,2,1:T(8,128)S(1)} %get-tuple-element.26), channel_id=1, source_target_pairs={{0,16},{16,32},{32,48},{48,64},{64,80},{80,96},{96,112},{1,17},{17... | collective-permute-start | bytes 786440 | tf_op jit(solution)/shard_map/ppermute | solution.py:15
  108.5 10.2 %collective-permute-start.14 = (f32[32,18,1,128]{3,0,2,1:T(8,128)S(1)}, f32[32,18,1,128]{3,0,2,1:T(8,128)S(1)}, u32[]{:S(2)}, u32[]{:S(2)}) collective-permute-start(f32[32,18,1,128]{3,0,2,1:T(8,128)S(1)} %get-tuple-element.16), channel_id=1, source_target_pairs={{2,0},{4,2},{6,4},{8,6},{10,8},{12,10},{14,12},{3,1},{5,3},{7,5},{... | collective-permute-start | bytes 884744 | tf_op jit(solution)/shard_map/ppermute | solution.py:18
  109.8 10.1 %collective-permute-start.15 = (f32[32,18,1,128]{3,0,2,1:T(8,128)S(1)}, f32[32,18,1,128]{3,0,2,1:T(8,128)S(1)}, u32[]{:S(2)}, u32[]{:S(2)}) collective-permute-start(f32[32,18,1,128]{3,0,2,1:T(8,128)S(1)} %get-tuple-element.17), channel_id=1, source_target_pairs={{0,2},{2,4},{4,6},{6,8},{8,10},{10,12},{12,14},{1,3},{3,5},{5,7},{... | collective-permute-start | bytes 884744 | tf_op jit(solution)/shard_map/ppermute | solution.py:15
  128.0 8.3 %collective-permute-start.16 = (f32[32,1,16,128]{3,0,2,1:T(8,128)S(1)}, f32[32,1,16,128]{3,0,2,1:T(8,128)S(1)}, u32[]{:S(2)}, u32[]{:S(2)}) collective-permute-start(f32[32,1,16,128]{3,0,2,1:T(8,128)S(1)} %get-tuple-element.25), channel_id=1, source_target_pairs={{16,0},{32,16},{48,32},{64,48},{80,64},{96,80},{112,96},{17,1},{33... | collective-permute-start | bytes 786440 | tf_op jit(solution)/shard_map/ppermute | solution.py:18
  129.9 11.9 %collective-permute-start.17 = (f32[32,1,16,128]{3,0,2,1:T(8,128)S(1)}, f32[32,1,16,128]{3,0,2,1:T(8,128)S(1)}, u32[]{:S(2)}, u32[]{:S(2)}) collective-permute-start(f32[32,1,16,128]{3,0,2,1:T(8,128)S(1)} %get-tuple-element.24), channel_id=1, source_target_pairs={{0,16},{16,32},{32,48},{48,64},{64,80},{80,96},{96,112},{1,17},{17... | collective-permute-start | bytes 786440 | tf_op jit(solution)/shard_map/ppermute | solution.py:15
  141.8 9.9 %collective-permute-start.18 = (f32[32,18,1,128]{3,0,2,1:T(8,128)S(1)}, f32[32,18,1,128]{3,0,2,1:T(8,128)S(1)}, u32[]{:S(2)}, u32[]{:S(2)}) collective-permute-start(f32[32,18,1,128]{3,0,2,1:T(8,128)S(1)} %get-tuple-element.14), channel_id=1, source_target_pairs={{2,0},{4,2},{6,4},{8,6},{10,8},{12,10},{14,12},{3,1},{5,3},{7,5},{... | collective-permute-start | bytes 884744 | tf_op jit(solution)/shard_map/ppermute | solution.py:18
  143.1 9.8 %collective-permute-start.19 = (f32[32,18,1,128]{3,0,2,1:T(8,128)S(1)}, f32[32,18,1,128]{3,0,2,1:T(8,128)S(1)}, u32[]{:S(2)}, u32[]{:S(2)}) collective-permute-start(f32[32,18,1,128]{3,0,2,1:T(8,128)S(1)} %get-tuple-element.15), channel_id=1, source_target_pairs={{0,2},{2,4},{4,6},{6,8},{8,10},{10,12},{12,14},{1,3},{3,5},{5,7},{... | collective-permute-start | bytes 884744 | tf_op jit(solution)/shard_map/ppermute | solution.py:15
  164.8 6.8 %copy-start.5 = (bf16[64,16,16,128]{3,2,1,0:T(8,128)(2,1)S(1)}, bf16[64,16,16,128]{3,2,1,0:T(8,128)(2,1)}, u32[]{:S(2)}) copy-start(bf16[64,16,16,128]{3,2,1,0:T(8,128)(2,1)} %param.9) | copy-start | bytes 12582916
  171.6 104.3 %copy-start.4 = (f32[64,32]{0,1:T(8,128)S(1)}, f32[64,32]{0,1:T(8,128)}, u32[]{:S(2)}) copy-start(f32[64,32]{0,1:T(8,128)} %param.11) | copy-start | bytes 24580
  281.4 1.6 copy-start.3
Sparse Core Ops, SparseCore 0:
  164.9 63.2 all-gather.3
